TPU v7x, 512 devices: a whole 4x8x8 slice. The times are simulated.
512 devices in a mesh: dp: 16 (over z_lo, y), mp: 8 (over z_hi, core), section: 4 (over x).
Axes of the slice: x: 4, y: 8, z: 8 (z_hi: 4, z_lo: 2; z = z_hi * 2 + z_lo), core: 2. Of those that a mesh axis runs over, the one named last changes fastest.
Arguments:
- states: bfloat16 [16384, 8192], P(('dp', 'section'), 'mp'), may hold values from -6 to 6
- direction: bfloat16 [16384, 1024], P(('dp', 'section'), 'mp'), may hold values from -0.09375 to 0.09375
- old_logp: bfloat16 [16384], P(('dp', 'section')), may hold values from -4 to -0.049804688
- lengths: int32 [128], P(('dp', 'section')), may hold values from 1 to 128, as said below
- group_ids: int32 [128], P(('dp', 'section')), may hold values from 0 to 15, as said below
- routes: int32 [16384, 1], P(('dp', 'section')), may hold values from 0 to 15; in each aligned block of 256 rows (0 to 255, 256 to 511, ...) at most 20 rows name the same one
- reward_head: bfloat16 [8192], P('mp'), may hold values from -0.0625 to 0.0625
- policy_k: bfloat16 [8192, 1024], P(('dp', 'section'), 'mp'), may hold values from -0.0625 to 0.0625
- reference_k: bfloat16 [8192, 1024], P(('dp', 'section'), 'mp'), may hold values from -0.0625 to 0.0625
Outputs:
- grad_k: float32 [8192, 1024], P(('dp', 'section'), 'mp')
- packed_logp: float32 [16, 4, 320], P('dp', 'section')
Inputs may be any that keep to these rules, and one draw needn't show every extreme that they name: `lengths`: some response has all 128 tokens valid. `group_ids`: each prompt id is held by exactly 8 responses. `routes`: among the rows of one rollout device at most 20 name the same learner shard, a bound that some block reaches of them.
All inputs are finite; a program needn't handle non-finite values.
Results may differ from a plain program's by a relative error of at most 0.004.
Values may be sent and summed in bfloat16 or wider, within the bound.
No kernel may reach another device: no remote copies, remote signals or barrier semaphores. Data moves between devices by JAX's collectives and lax.ppermute only.
A program may use at most 64 MiB of HBM per device.

v0:
```python
import jax
import jax.numpy as jnp
from jax import lax
from jax.sharding import PartitionSpec as P

GROUP = 8
kl_weight = 0.4
var_offset = 0.25


def row_slots(routes, shards, capacity):
    target = routes[:, 0]
    choose = (target[:, None] == jnp.arange(shards, dtype=jnp.int32)[None, :]).astype(jnp.int32)
    ranked = jnp.cumsum(choose, axis=0) - 1
    within = jnp.sum(ranked * choose, axis=1)
    places = target * capacity + within
    row_count = routes.shape[0]
    source = jnp.full((shards * capacity,), row_count, jnp.int32)
    return source.at[places].set(jnp.arange(row_count, dtype=jnp.int32))


def pick_rows(values, source):
    return jnp.take(values, source, axis=0, mode="fill", fill_value=0)


def advantages(scores, lengths, group_ids):
    seq_count = lengths.shape[0]
    seq_len = scores.shape[0] // seq_count
    groups = seq_count * lax.axis_size("dp") * lax.axis_size("section") // GROUP
    valid = (jnp.arange(seq_len, dtype=jnp.int32)[None, :] < lengths[:, None]).astype(jnp.float32)
    reward = jnp.sum(scores.reshape(seq_count, seq_len) * valid, axis=1) / jnp.sqrt(
        lengths.astype(jnp.float32)
    )
    member = (group_ids[:, None] == jnp.arange(groups, dtype=jnp.int32)[None, :]).astype(
        jnp.float32
    )
    totals, squares = lax.psum(
        (
            jnp.sum(member * reward[:, None], axis=0),
            jnp.sum(member * (reward * reward)[:, None], axis=0),
        ),
        ("dp", "section"),
    )
    center = totals / GROUP
    spread = squares / GROUP - center * center
    own_center = jnp.sum(member * center[None, :], axis=1)
    own_spread = jnp.sum(member * spread[None, :], axis=1)
    advantage = ((reward - own_center) / jnp.sqrt(own_spread + var_offset)).astype(jnp.bfloat16)
    return (jnp.repeat(advantage, seq_len), valid.reshape(-1))


def project(whole, policy_k, reference_k):
    return (
        jnp.dot(
            whole,
            lax.all_gather(policy_k, ("dp", "section"), axis=0, tiled=True),
            preferred_element_type=jnp.float32,
        ),
        jnp.dot(
            whole,
            lax.all_gather(reference_k, ("dp", "section"), axis=0, tiled=True),
            preferred_element_type=jnp.float32,
        ),
    )


def token_coef(dir_rows, old_rows, adv_rows, valid_rows, term_policy, term_reference):
    logp = old_rows.astype(jnp.float32) + term_policy
    coef = valid_rows * (
        -adv_rows * jnp.exp(term_policy) + kl_weight * (1.0 - jnp.exp(term_reference - term_policy))
    )
    change = (coef[:, None] * dir_rows.astype(jnp.float32)).astype(jnp.bfloat16)
    return (logp, change)


def weight_grads(whole, change):
    return lax.psum_scatter(
        lax.dot_general(
            whole, change, (((0,), (0,)), ((), ())), preferred_element_type=jnp.float32
        ),
        ("dp", "section"),
        scatter_dimension=0,
        tiled=True,
    )


def body(
    states, direction, old_logp, lengths, group_ids, routes, reward_head, policy_k, reference_k
):
    row_count = states.shape[0]
    score_part = jnp.dot(states, reward_head, preferred_element_type=jnp.float32)
    shards = lax.axis_size("dp")
    capacity = max(2, 5 * row_count // (4 * shards))
    source = row_slots(routes, shards, capacity)
    scores = lax.psum(score_part, "mp")
    adv_rows, valid_rows = advantages(scores, lengths, group_ids)
    extras = jnp.stack([old_logp, adv_rows, valid_rows.astype(jnp.bfloat16)], axis=1)
    send_states = pick_rows(states, source).reshape(shards, capacity, states.shape[1])
    send_dir = pick_rows(direction, source).reshape(shards, capacity, direction.shape[1])
    send_extras = pick_rows(extras, source).reshape(shards, capacity, 3)
    got_states, got_dir, got_extras = (
        lax.all_to_all(send_states, "dp", split_axis=0, concat_axis=0, tiled=True),
        lax.all_to_all(send_dir, "dp", split_axis=0, concat_axis=0, tiled=True),
        lax.all_to_all(send_extras, "dp", split_axis=0, concat_axis=0, tiled=True),
    )
    slot_count = shards * capacity
    learn_states = got_states.reshape(slot_count, states.shape[1])
    learn_dir = got_dir.reshape(slot_count, direction.shape[1])
    learn_extras = got_extras.reshape(slot_count, 3)
    whole = lax.all_gather(learn_states, "mp", axis=1, tiled=True)
    key_policy, key_reference = project(whole, policy_k, reference_k)
    dir_wide = learn_dir.astype(jnp.float32)
    term_policy, term_reference = lax.psum(
        (jnp.sum(dir_wide * key_policy, axis=1), jnp.sum(dir_wide * key_reference, axis=1)), "mp"
    )
    logp, change = token_coef(
        learn_dir,
        learn_extras[:, 0],
        learn_extras[:, 1].astype(jnp.float32),
        learn_extras[:, 2].astype(jnp.float32),
        term_policy,
        term_reference,
    )
    grad_k = weight_grads(whole, change)
    packed_logp = logp.reshape(1, 1, slot_count)
    return (grad_k, packed_logp)


def solution(mesh):
    return jax.shard_map(
        body,
        mesh=mesh,
        in_specs=(
            P(("dp", "section"), "mp"),
            P(("dp", "section"), "mp"),
            P(("dp", "section")),
            P(("dp", "section")),
            P(("dp", "section")),
            P(("dp", "section"), None),
            P("mp"),
            P(("dp", "section"), "mp"),
            P(("dp", "section"), "mp"),
        ),
        out_specs=(P(("dp", "section"), "mp"), P("dp", "section", None)),
        check_vma=False,
    )
```

profile of v0, /device:TPU:64, one launch (start us, length us, event | category | flops | bytes accessed | tf_op | source)
XLA Modules:
  0.0 1203.8 jit_solution(4523003245266882236)
XLA Ops:
  7.2 0.7 all-gather.6.cloned.1.call-update
  8.0 0.7 fusion.6
  9.4 0.8 fusion.5
  10.2 0.7 compare_select_fusion
  10.9 1.4 scatter_custom_fusion
  12.4 2.1 gather_fusion
  14.9 29.1 %all_to_all.15 = bf16[16,20,1024]{2,1,0:T(8,128)(2,1)S(1)} all-to-all(bf16[16,20,1024]{2,1,0:T(8,128)(2,1)S(1)} %broadcast_select_fusion), channel_id=1, replica_groups=mesh['dp'=16,'mp'=8,'section'=4] {'dp'}, dimensions={0} | all-to-all | bytes 1310720 | tf_op jit(solution)/shard_map/all_to_all | solution.py:102
  44.0 1.0 reshape.105
  45.0 0.7 all-gather.8.cloned.1.call-update
  45.7 1.4 gather_fusion.2
  47.2 0.8 broadcast_select_fusion.1
  47.9 6.3 all-to-all-start.2
  54.7 7.0 all-to-all-done.2
  61.7 253.6 %all-gather.6.cloned.1.call-done = bf16[8192,128]{1,0:T(8,128)(2,1)} async-done(((bf16[128,128]{1,0:T(8,128)(2,1)}), bf16[8192,128]{1,0:T(8,128)(2,1)}) %all-gather.6.cloned.1.call-update) | async-done | bytes 2097168 | tf_op jit(solution)/shard_map/all_gather | solution.py:56
  315.3 65.4 %all-gather.4.cloned.1.call-done = bf16[320,8192]{1,0:T(8,128)(2,1)} async-done(((bf16[320,1024]{1,0:T(8,128)(2,1)}), bf16[320,8192]{1,0:T(8,128)(2,1)}) %all-gather.4.cloned.1.call-update) | async-done | bytes 5242896 | tf_op jit(solution)/shard_map/all_gather | solution.py:110
  380.7 4.8 fusion
  385.5 297.1 %all-gather.8.cloned.1.call-done = bf16[8192,128]{1,0:T(8,128)(2,1)} async-done(((bf16[128,128]{1,0:T(8,128)(2,1)}), bf16[8192,128]{1,0:T(8,128)(2,1)}) %all-gather.8.cloned.1.call-update) | async-done | bytes 2097168 | tf_op jit(solution)/shard_map/all_gather | solution.py:61
  682.6 4.8 fusion.1
  687.4 14.7 %all-reduce.1 = (f32[2,128]{1,0:T(2,128)S(1)}, f32[320]{0:T(512)S(1)}, f32[320]{0:T(512)S(1)}) all-reduce(f32[2,128]{1,0:T(2,128)S(1)} %bitcast.47, f32[320]{0:T(512)S(1)} %fusion.1, f32[320]{0:T(512)S(1)} %fusion), channel_id=1, replica_groups=mesh['dp'=16,'mp'=8,'section'=4] {'mp'}, use_global_device_ids=true, to_apply=%region_4.5 | all-reduce | flops 896 | bytes 7168 | tf_op jit(solution)/shard_map/psum | solution.py:95
  702.4 157.2 %all-reduce = (f32[16]{0:T(128)S(1)}, f32[16]{0:T(128)S(1)}) all-reduce(f32[16]{0:T(128)S(1)} %get-tuple-element.7, f32[16]{0:T(128)S(1)} %get-tuple-element.8), channel_id=1, replica_groups=mesh['dp'=16,'mp'=8,'section'=4] {'dp','section'}, use_global_device_ids=true, to_apply=%region_7.8 | all-reduce | flops 32 | bytes 256 | tf_op jit(solution)/shard_map/psum | solution.py:37
  860.1 1.4 gather_fusion.1
  861.7 10.8 all_to_all.16
  872.7 6.5 fusion.2
  879.7 317.5 %reduce-scatter.2.cloned.1.call-done = f32[128,128]{1,0:T(8,128)} async-done(((f32[8192,128]{1,0:T(8,128)}), f32[128,128]{1,0:T(8,128)}) %reduce-scatter.2.cloned.1.call-update) | async-done | bytes 65552 | tf_op jit(solution)/shard_map/reduce_scatter | solution.py:77
  (54 shorter events, 3.4 us)
Async XLA Ops:
  7.2 5.2 copy-start
  7.2 308.1 %all-gather.6.cloned.1.call-start = ((), (), s32[]{:S(2)}) async-start(), calls=%async_computation.5 | async-start | bytes 2129920 | tf_op jit(solution)/shard_map/all_gather | solution.py:56
  7.9 372.8 %all-gather.4.cloned.1.call-start = ((), (), s32[]{:S(2)}) async-start(), calls=%async_computation.4 | async-start | bytes 5898240 | tf_op jit(solution)/shard_map/all_gather | solution.py:110
  12.3 33.4 %copy-start.1 = (bf16[256,128]{1,0:T(8,128)(2,1)S(1)}, bf16[256,128]{1,0:T(8,128)(2,1)}, u32[]{:S(2)}) copy-start(bf16[256,128]{1,0:T(8,128)(2,1)} %param.10) | copy-start | bytes 196612
  14.5 39.9 %copy-start.2 = (bf16[1024]{0:T(1024)(128)(2,1)S(1)}, bf16[1024]{0:T(1024)(128)(2,1)}, u32[]{:S(2)}) copy-start(bf16[1024]{0:T(1024)(128)(2,1)} %param.15) | copy-start | bytes 6148
  14.5 39.9 %copy-start.5 = (bf16[256]{0:T(256)(128)(2,1)S(1)}, bf16[256]{0:T(256)(128)(2,1)}, u32[]{:S(2)}) copy-start(bf16[256]{0:T(256)(128)(2,1)} %param.11) | copy-start | bytes 1540
  14.5 40.1 %copy-start.4 = (s32[2]{0:T(128)S(1)}, s32[2]{0:T(128)}, u32[]{:S(2)}) copy-start(s32[2]{0:T(128)} %param.12) | copy-start | bytes 28
  45.0 637.6 %all-gather.8.cloned.1.call-start = ((), (), s32[]{:S(2)}) async-start(), calls=%async_computation.6 | async-start | bytes 2129920 | tf_op jit(solution)/shard_map/all_gather | solution.py:61
  47.9 13.8 %all-to-all-start.2 = ((bf16[16,20,128]{2,1,0:T(8,128)(2,1)}), bf16[16,20,128]{2,1,0:T(8,128)(2,1)S(1)}, u32[]{:S(2)}, u32[]{:S(2)}) async-start(bf16[16,20,128]{2,1,0:T(8,128)(2,1)} %broadcast_select_fusion.1), calls=%async_computation.2 | async-start | bytes 196608 | tf_op jit(solution)/shard_map/all_to_all | solution.py:103
  54.3 1143.0 %reduce-scatter.2.cloned.1.call-start = ((), (), s32[]{:S(2)}) async-start(), calls=%async_computation.7 | async-start | bytes 4259840 | tf_op jit(solution)/shard_map/reduce_scatter | solution.py:77
  385.5 316.8 %copy-start.3 = (s32[2]{0:T(128)S(1)}, s32[2]{0:T(128)}, u32[]{:S(2)}) copy-start(s32[2]{0:T(128)} %param.13) | copy-start | bytes 28
Sparse Core Ops, SparseCore 0:
  10.1 305.1 all-gather.5
  317.4 63.2 all-gather.3
  382.8 299.7 all-gather.7
  879.3 317.9 reduce-scatter.1
where the time goes:
time: 1200 us
  waiting for transfers between devices  942 us (78%)
  blocking collectives  212 us (18%)
  matrix products  16.2 us (1%)
  between operations  14 us (1%)
    reduce_scatter x1, waiting for transfers between devices, weight_grads(): lax.psum_scatter(lax.dot_general(whole, change, (((0,), (0,)), ((), ())),...  318 us
    all_gather x1, waiting for transfers between devices, project(): lax.all_gather(reference_k, ('dp', 'section'), axis=0, tiled=True)  297 us
    all_gather x1, waiting for transfers between devices, project(): lax.all_gather(policy_k, ('dp', 'section'), axis=0, tiled=True)  254 us
    psum x1, blocking collectives, advantages(): lax.psum((jnp.sum(member * reward[:, None], axis=0), jnp.sum(member * (re...  157 us
    all_gather x1, waiting for transfers between devices, body(): whole = lax.all_gather(learn_states, 'mp', axis=1, tiled=True)  65.4 us
    all_to_all x1, blocking collectives, body(): lax.all_to_all(send_states, 'dp', split_axis=0, concat_axis=0, tiled=True)  29.1 us
  transfers between devices with their start and end apart: 5, of which 5 were waited for; matrix products, arithmetic and copies ran while one was open for 1% of the time, Pallas kernels for 0%

commit v1 on v0

--- a/solution.py
+++ b/solution.py
@@ -34,12 +34,18 @@
     member = (group_ids[:, None] == jnp.arange(groups, dtype=jnp.int32)[None, :]).astype(
         jnp.float32
     )
-    totals, squares = lax.psum(
+
+    def orders_switch(xin, group_axis, axis_key):
+        aux = lax.psum(lax.psum(xin, axis_name=group_axis), axis_name=axis_key)
+        return aux
+
+    totals, squares = orders_switch(
         (
             jnp.sum(member * reward[:, None], axis=0),
             jnp.sum(member * (reward * reward)[:, None], axis=0),
         ),
-        ("dp", "section"),
+        "dp",
+        axis_key="section",
     )
     center = totals / GROUP
     spread = squares / GROUP - center * center

time: 1200 us -> 1090 us (0.908)
  the two profiles are of different devices: /device:TPU:64 before, /device:TPU:128 now
where the time goes in v1:
time: 1090 us
  waiting for transfers between devices  944 us (87%)
  blocking collectives  97.5 us (9%)
  matrix products  16.2 us (1%)
  between operations  14 us (1%)
    reduce_scatter x1, waiting for transfers between devices, weight_grads(): lax.psum_scatter(lax.dot_general(whole, change, (((0,), (0,)), ((), ())),...  320 us
    all_gather x1, waiting for transfers between devices, project(): lax.all_gather(reference_k, ('dp', 'section'), axis=0, tiled=True)  298 us
    all_gather x1, waiting for transfers between devices, project(): lax.all_gather(policy_k, ('dp', 'section'), axis=0, tiled=True)  253 us
    all_gather x1, waiting for transfers between devices, body(): whole = lax.all_gather(learn_states, 'mp', axis=1, tiled=True)  64.4 us
    psum x2, blocking collectives, orders_switch(): aux = lax.psum(lax.psum(xin, axis_name=group_axis), axis_name=axis_key)  43.6 us
    all_to_all x1, blocking collectives, body(): lax.all_to_all(send_states, 'dp', split_axis=0, concat_axis=0, tiled=True)  30.2 us
  transfers between devices with their start and end apart: 5, of which 5 were waited for; matrix products, arithmetic and copies ran while one was open for 1% of the time, Pallas kernels for 0%

profile of v1, /device:TPU:128, one launch (start us, length us, event | category | flops | bytes accessed | tf_op | source)
XLA Modules:
  0.0 1091.2 jit_solution(8957405272188049484)
XLA Ops:
  7.2 0.7 all-gather.6.cloned.1.call-update
  8.0 0.7 fusion.6
  9.4 0.8 fusion.5
  10.2 0.7 compare_select_fusion
  10.9 1.4 scatter_custom_fusion
  12.4 2.1 gather_fusion
  14.9 30.2 %all_to_all.15 = bf16[16,20,1024]{2,1,0:T(8,128)(2,1)S(1)} all-to-all(bf16[16,20,1024]{2,1,0:T(8,128)(2,1)S(1)} %broadcast_select_fusion), channel_id=1, replica_groups=mesh['dp'=16,'mp'=8,'section'=4] {'dp'}, dimensions={0} | all-to-all | bytes 1310720 | tf_op jit(solution)/shard_map/all_to_all | solution.py:108
  45.1 1.0 reshape.105
  46.8 1.4 gather_fusion.2
  48.3 0.8 broadcast_select_fusion.1
  49.0 5.9 all-to-all-start.2
  55.3 8.2 all-to-all-done.2
  63.5 252.7 %all-gather.6.cloned.1.call-done = bf16[8192,128]{1,0:T(8,128)(2,1)} async-done(((bf16[128,128]{1,0:T(8,128)(2,1)}), bf16[8192,128]{1,0:T(8,128)(2,1)}) %all-gather.6.cloned.1.call-update) | async-done | bytes 2097168 | tf_op jit(solution)/shard_map/all_gather | solution.py:62
  316.1 64.4 %all-gather.4.cloned.1.call-done = bf16[320,8192]{1,0:T(8,128)(2,1)} async-done(((bf16[320,1024]{1,0:T(8,128)(2,1)}), bf16[320,8192]{1,0:T(8,128)(2,1)}) %all-gather.4.cloned.1.call-update) | async-done | bytes 5242896 | tf_op jit(solution)/shard_map/all_gather | solution.py:116
  380.6 4.8 fusion
  385.4 297.6 %all-gather.8.cloned.1.call-done = bf16[8192,128]{1,0:T(8,128)(2,1)} async-done(((bf16[128,128]{1,0:T(8,128)(2,1)}), bf16[8192,128]{1,0:T(8,128)(2,1)}) %all-gather.8.cloned.1.call-update) | async-done | bytes 2097168 | tf_op jit(solution)/shard_map/all_gather | solution.py:67
  683.0 4.8 fusion.1
  687.8 12.6 %all-reduce.1 = (f32[2,128]{1,0:T(2,128)S(1)}, f32[320]{0:T(512)S(1)}, f32[320]{0:T(512)S(1)}) all-reduce(f32[2,128]{1,0:T(2,128)S(1)} %bitcast.47, f32[320]{0:T(512)S(1)} %fusion.1, f32[320]{0:T(512)S(1)} %fusion), channel_id=1, replica_groups=mesh['dp'=16,'mp'=8,'section'=4] {'mp'}, use_global_device_ids=true, to_apply=%region_4.5 | all-reduce | flops 896 | bytes 7168 | tf_op jit(solution)/shard_map/psum | solution.py:101
  700.7 30.6 %all-reduce = (f32[16]{0:T(128)S(1)}, f32[16]{0:T(128)S(1)}) all-reduce(f32[16]{0:T(128)S(1)} %get-tuple-element.7, f32[16]{0:T(128)S(1)} %get-tuple-element.8), channel_id=1, replica_groups=mesh['dp'=16,'mp'=8,'section'=4] {'dp'}, use_global_device_ids=true, to_apply=%region_7.8 | all-reduce | flops 32 | bytes 256 | tf_op jit(solution)/shard_map/psum | solution.py:39
  731.3 13.0 %all-reduce.2 = (f32[16]{0:T(128)S(1)}, f32[16]{0:T(128)S(1)}) all-reduce(f32[16]{0:T(128)S(1)} %get-tuple-element.9, f32[16]{0:T(128)S(1)} %get-tuple-element.10), channel_id=1, replica_groups=mesh['dp'=16,'mp'=8,'section'=4] {'section'}, use_global_device_ids=true, to_apply=%region_8.9 | all-reduce | flops 32 | bytes 256 | tf_op jit(solution)/shard_map/psum | solution.py:39
  744.8 1.4 gather_fusion.1
  746.4 11.0 %all_to_all.16 = bf16[16,20,3]{1,2,0:T(4,128)(2,1)S(1)} all-to-all(bf16[16,20,3]{1,2,0:T(4,128)(2,1)S(1)} %copy.24), channel_id=1, replica_groups=mesh['dp'=16,'mp'=8,'section'=4] {'dp'}, dimensions={0} | all-to-all | bytes 3840 | tf_op jit(solution)/shard_map/all_to_all | solution.py:110
  757.6 6.5 fusion.2
  764.7 320.0 %reduce-scatter.2.cloned.1.call-done = f32[128,128]{1,0:T(8,128)} async-done(((f32[8192,128]{1,0:T(8,128)}), f32[128,128]{1,0:T(8,128)}) %reduce-scatter.2.cloned.1.call-update) | async-done | bytes 65552 | tf_op jit(solution)/shard_map/reduce_scatter | solution.py:83
  (55 shorter events, 4.1 us)
Async XLA Ops:
  7.2 5.2 copy-start
  7.2 309.0 %all-gather.6.cloned.1.call-start = ((), (), s32[]{:S(2)}) async-start(), calls=%async_computation.5 | async-start | bytes 2129920 | tf_op jit(solution)/shard_map/all_gather | solution.py:62
  7.9 372.7 %all-gather.4.cloned.1.call-start = ((), (), s32[]{:S(2)}) async-start(), calls=%async_computation.4 | async-start | bytes 5898240 | tf_op jit(solution)/shard_map/all_gather | solution.py:116
  12.3 34.5 %copy-start.1 = (bf16[256,128]{1,0:T(8,128)(2,1)S(1)}, bf16[256,128]{1,0:T(8,128)(2,1)}, u32[]{:S(2)}) copy-start(bf16[256,128]{1,0:T(8,128)(2,1)} %param.10) | copy-start | bytes 196612
  14.5 40.5 %copy-start.2 = (bf16[1024]{0:T(1024)(128)(2,1)S(1)}, bf16[1024]{0:T(1024)(128)(2,1)}, u32[]{:S(2)}) copy-start(bf16[1024]{0:T(1024)(128)(2,1)} %param.15) | copy-start | bytes 6148
  14.5 40.5 %copy-start.5 = (bf16[256]{0:T(256)(128)(2,1)S(1)}, bf16[256]{0:T(256)(128)(2,1)}, u32[]{:S(2)}) copy-start(bf16[256]{0:T(256)(128)(2,1)} %param.11) | copy-start | bytes 1540
  14.5 40.8 %copy-start.4 = (s32[2]{0:T(128)S(1)}, s32[2]{0:T(128)}, u32[]{:S(2)}) copy-start(s32[2]{0:T(128)} %param.12) | copy-start | bytes 28
  46.1 636.9 %all-gather.8.cloned.1.call-start = ((), (), s32[]{:S(2)}) async-start(), calls=%async_computation.6 | async-start | bytes 2129920 | tf_op jit(solution)/shard_map/all_gather | solution.py:67
  49.0 14.5 %all-to-all-start.2 = ((bf16[16,20,128]{2,1,0:T(8,128)(2,1)}), bf16[16,20,128]{2,1,0:T(8,128)(2,1)S(1)}, u32[]{:S(2)}, u32[]{:S(2)}) async-start(bf16[16,20,128]{2,1,0:T(8,128)(2,1)} %broadcast_select_fusion.1), calls=%async_computation.2 | async-start | bytes 196608 | tf_op jit(solution)/shard_map/all_to_all | solution.py:109
  54.9 1029.7 %reduce-scatter.2.cloned.1.call-start = ((), (), s32[]{:S(2)}) async-start(), calls=%async_computation.7 | async-start | bytes 4259840 | tf_op jit(solution)/shard_map/reduce_scatter | solution.py:83
  385.4 315.2 %copy-start.3 = (s32[2]{0:T(128)S(1)}, s32[2]{0:T(128)}, u32[]{:S(2)}) copy-start(s32[2]{0:T(128)} %param.13) | copy-start | bytes 28
Sparse Core Ops, SparseCore 0:
  10.1 305.9 all-gather.5
  318.3 62.2 all-gather.3
  382.7 300.2 all-gather.7
  764.2 320.3 reduce-scatter.1
